TPU v7x, 32 devices: a whole 2x2x4 slice. The times are simulated.
32 devices in a mesh: row: 8 (over z, y), col: 4 (over x, core).
Axes of the slice: x: 2, y: 2, z: 4, core: 2. Of those that a mesh axis runs over, the one named last changes fastest.
Arguments:
- front: bfloat16 [2, 16384, 3072], P(None, 'row', 'col'), may hold values from -6 to 6
- child_tiles: bfloat16 [4096, 2, 128, 128], P(('row', 'col')), may hold values from -6 to 6
- tile_owner: int32 [4096, 1], P(('row', 'col')), may hold values from 0 to 31; in each aligned block of 128 rows (0 to 127, 128 to 255, ...) at most 8 rows name the same one
- tile_spot: int32 [4096], P(('row', 'col')), may hold values from 0 to 95
- tile_count: int32 [32], P(('row', 'col')), may hold values from 96 to 128, as said below
- panel: bfloat16 [2, 16384, 512], P(None, 'row'), may hold values from -0.03125 to 0.03125
Outputs:
- assembled: bfloat16 [2, 16384, 3072], P(None, 'row', 'col')
- sample: float32 [2, 512, 3072], P(None, 'row', 'col')
Inputs may be any that keep to these rules, and one draw needn't show every extreme that they name: `tile_owner`: among the 128 tiles of one device, at most 8 name the same owner. `tile_count`: some device holds 128 live tiles.
All inputs are finite; a program needn't handle non-finite values.
Results may differ from a plain program's by a relative error of at most 0.0042.
Values may be sent and summed in bfloat16 or wider, within the bound.
A program may use at most 256 MiB of HBM per device.

v0:
```python
import jax
import jax.numpy as jnp
from jax import lax
from jax.sharding import PartitionSpec as P


def body(front, child_tiles, tile_owner, tile_spot, tile_count, panel):
    n_row = lax.axis_size("row")
    n_col = lax.axis_size("col")
    n_dev = n_row * n_col
    n_tiles = child_tiles.shape[0]
    tile = child_tiles.shape[2]
    slots = max(2, 2 * n_tiles // n_dev)
    rows_blocks = front.shape[1] // tile
    cols_blocks = front.shape[2] // tile
    n_local = rows_blocks * cols_blocks
    order = jnp.arange(n_tiles, dtype=jnp.int32)
    owner = tile_owner[:, 0]
    live = order < tile_count[0]
    earlier = (owner[:, None] == owner[None, :]) & live[None, :] & (order[None, :] < order[:, None])
    rank = jnp.sum(earlier.astype(jnp.int32), axis=1)
    slot = jnp.where(live, owner * slots + rank, n_dev * slots)
    source = jnp.full((n_dev * slots,), n_tiles, jnp.int32).at[slot].set(order, mode="drop")
    filled = source < n_tiles
    picked = jnp.minimum(source, n_tiles - 1)
    send_tiles = child_tiles[picked]
    send_spots = jnp.where(filled, tile_spot[picked], n_local)
    got_tiles, got_spots = (
        lax.all_to_all(
            send_tiles.reshape(n_dev, slots, 2, tile, tile),
            ("row", "col"),
            split_axis=0,
            concat_axis=0,
            tiled=True,
        ),
        lax.all_to_all(
            send_spots.reshape(n_dev, slots),
            ("row", "col"),
            split_axis=0,
            concat_axis=0,
            tiled=True,
        ),
    )
    got_tiles = got_tiles.reshape(n_dev * slots, 2, tile, tile)
    got_spots = got_spots.reshape(n_dev * slots)
    accum = front.astype(jnp.float32).reshape(2, rows_blocks, tile, cols_blocks, tile)
    selector = (got_spots[None, :] == jnp.arange(n_local, dtype=jnp.int32)[:, None]).astype(
        jnp.bfloat16
    )
    summed = jnp.dot(
        selector,
        got_tiles.reshape(n_dev * slots, 2 * tile * tile),
        preferred_element_type=jnp.float32,
    )
    summed = summed.reshape(rows_blocks, cols_blocks, 2, tile, tile).transpose(2, 0, 3, 1, 4)
    accum = accum + summed
    assembled = accum.reshape(2, rows_blocks * tile, cols_blocks * tile).astype(jnp.bfloat16)
    width = cols_blocks * tile
    stacked = jnp.concatenate([assembled[0], assembled[1]], axis=1)
    panel_re = panel[0]
    panel_im = panel[1]
    rows_out = panel.shape[2] // n_row
    from_re = lax.dot_general(
        panel_re, stacked, (((0,), (0,)), ((), ())), preferred_element_type=jnp.float32
    )
    from_im = lax.dot_general(
        panel_im, stacked, (((0,), (0,)), ((), ())), preferred_element_type=jnp.float32
    )
    real_part = from_re[:, :width] + from_im[:, width:]
    imag_part = from_re[:, width:] - from_im[:, :width]
    mine = lax.psum_scatter(
        jnp.concatenate([real_part, imag_part], axis=1), "row", scatter_dimension=0, tiled=True
    )
    sample = mine.reshape(rows_out, 2, width).transpose(1, 0, 2)
    return (assembled, sample)


def solution(mesh):
    placed = (
        P(None, "row", "col"),
        P(("row", "col"), None, None, None),
        P(("row", "col"), None),
        P(("row", "col")),
        P(("row", "col")),
        P(None, "row", None),
    )
    return jax.shard_map(
        body,
        mesh=mesh,
        in_specs=placed,
        out_specs=(P(None, "row", "col"), P(None, "row", "col")),
        check_vma=False,
    )
```

profile of v0, /device:TPU:0, one launch (start us, length us, event | category | flops | bytes accessed | tf_op | source)
XLA Modules:
  0.0 581.9 jit_solution(3122349126110872699)
XLA Ops:
  7.9 0.9 convert_reduce_fusion
  8.8 0.7 fusion.12
  9.4 1.0 scatter_custom_fusion
  10.5 1.9 gather_fusion
  12.3 0.7 all_to_all.9
  13.0 7.3 %all-to-all-start = ((s32[32,1,8]{2,1,0:T(1,128)}), s32[32,1,8]{2,1,0:T(1,128)S(1)}, u32[]{:S(2)}, u32[]{:S(2)}) async-start(s32[32,1,8]{2,1,0:T(1,128)} %bitcast.4), calls=%async_computation | async-start | bytes 32768 | tf_op jit(solution)/shard_map/all_to_all | solution.py:36
  20.4 12.8 %gather_fusion.1 = bf16[256,2,128,128]{3,2,1,0:T(8,128)(2,1)} fusion(bf16[128,2,128,128]{3,2,1,0:T(8,128)(2,1)} %param.7, s32[1024]{0:T(1024)S(1)} %pad_clamp_fusion), kind=kCustom, calls=%fused_computation.1 | custom fusion | bytes 33555456 | tf_op jit(solution)/shard_map/gather | solution.py:26
  33.2 6.0 %all-to-all-start.1 = ((bf16[32,8,2,128,128]{4,3,2,1,0:T(8,128)(2,1)}), bf16[32,8,2,128,128]{4,3,2,1,0:T(8,128)(2,1)}, u32[]{:S(2)}, u32[]{:S(2)}) async-start(bf16[32,8,2,128,128]{4,3,2,1,0:T(8,128)(2,1)} %bitcast.58), calls=%async_computation.1 | async-start | bytes 33554432 | tf_op jit(solution)/shard_map/all_to_all | solution.py:29
  39.2 14.8 %reshape.95 = f32[2,16,128,6,128]{4,3,2,1,0:T(8,128)} reshape(bf16[2,2048,768]{2,1,0:T(8,128)(2,1)} %param.6) | data formatting | bytes 18874368 | tf_op jit(solution)/shard_map/reshape | solution.py:46
  54.0 0.5 broadcast.55
  54.5 0.7 reduce.3
  55.3 356.5 %all-to-all-done.1 = bf16[32,8,2,128,128]{4,3,2,1,0:T(8,128)(2,1)} async-done(((bf16[32,8,2,128,128]{4,3,2,1,0:T(8,128)(2,1)}), bf16[32,8,2,128,128]{4,3,2,1,0:T(8,128)(2,1)}, u32[]{:S(2)}, u32[]{:S(2)}) %all-to-all-start.1) | async-done | bytes 16777248 | tf_op jit(solution)/shard_map/all_to_all | solution.py:29
  411.8 25.3 %reshape_reshape.3 = bf16[256,32768]{1,0:T(8,128)(2,1)} reshape(bf16[32,8,2,128,128]{4,3,2,1,0:T(8,128)(2,1)} %all-to-all-done.1) | data formatting | bytes 33554432 | tf_op jit(solution)/shard_map/reshape;reshape | solution.py:52
  437.1 22.4 %copy.29 = bf16[32768,256]{1,0:T(8,128)(2,1)} copy(bf16[32768,256]{0,1:T(8,128)(2,1)} %bitcast.59) | data formatting | bytes 33554432 | tf_op jit(solution)/shard_map/dot_general | solution.py:50
  459.5 12.9 %fusion = bf16[2,16,128,6,128]{4,1,2,0,3:T(8,128)(2,1)S(1)} fusion(f32[2,16,128,6,128]{4,3,2,1,0:T(8,128)} %reshape.95, bf16[2,128,128,256,1]{3,2,1,0,4:T(8,128)(2,1)} %bitcast.60, s32[16,6]{0,1:T(8,128)S(1)} %multiply_add_fusion, s32[256]{0:T(256)S(1)} %eq.45), kind=kOutput, calls=%fused_computation.4 | convolution fusion | flops 1616928768 | bytes 35652992 | tf_op jit(solution)/shard_map/dot_general | solution.py:50
  472.4 4.1 fusion.13
  476.4 0.5 copy-done.2
  476.9 4.5 copy.33
  481.5 5.4 copy.32
  486.9 2.9 bitcast_dynamic-update-slice_fusion.1
  489.8 0.8 bitcast_dynamic-update-slice_fusion
  490.6 1.4 copy-done.3
  492.0 3.4 convolution_bitcast_fusion
  495.4 3.4 convolution_bitcast_fusion.1
  498.9 0.7 slice_add_fusion
  499.6 0.3 pad_maximum_fusion
  500.0 2.5 copy.40
  502.4 10.3 %copy.39 = bf16[2,16,128,6,128]{4,3,2,1,0:T(8,128)(2,1)} copy(bf16[2,16,128,6,128]{4,1,2,0,3:T(8,128)(2,1)} %copy-done.2) | data formatting | bytes 12582912
  512.8 13.9 %reshape.96 = bf16[2,2048,768]{2,1,0:T(8,128)(2,1)} reshape(bf16[2,16,128,6,128]{4,3,2,1,0:T(8,128)(2,1)} %copy.39) | data formatting | bytes 12582912
  526.6 46.2 %reduce-scatter.4.cloned.1.call-done = f32[64,1536]{1,0:T(8,128)} async-done(((f32[512,1536]{1,0:T(8,128)}), f32[64,1536]{1,0:T(8,128)}) %reduce-scatter.4.cloned.1.call-update) | async-done | bytes 393232
  572.8 1.3 copy.41
  574.1 1.0 copy.34
  (16 shorter events, 0.2 us)
Async XLA Ops:
  7.2 3.3 copy-start
  13.0 20.1 %all-to-all-start = ((s32[32,1,8]{2,1,0:T(1,128)}), s32[32,1,8]{2,1,0:T(1,128)S(1)}, u32[]{:S(2)}, u32[]{:S(2)}) async-start(s32[32,1,8]{2,1,0:T(1,128)} %bitcast.4), calls=%async_computation | async-start | bytes 32768 | tf_op jit(solution)/shard_map/all_to_all | solution.py:36
  33.2 378.6 %all-to-all-start.1 = ((bf16[32,8,2,128,128]{4,3,2,1,0:T(8,128)(2,1)}), bf16[32,8,2,128,128]{4,3,2,1,0:T(8,128)(2,1)}, u32[]{:S(2)}, u32[]{:S(2)}) async-start(bf16[32,8,2,128,128]{4,3,2,1,0:T(8,128)(2,1)} %bitcast.58), calls=%async_computation.1 | async-start | bytes 33554432 | tf_op jit(solution)/shard_map/all_to_all | solution.py:29
  39.2 533.6 %reduce-scatter.4.cloned.1.call-start = ((), (), s32[]{:S(2)}) async-start(), calls=%async_computation.3 | async-start | bytes 3538944
  472.3 4.6 copy-start.2
  489.8 2.2 copy-start.3
  512.8 62.3 %copy-start.1 = (s32[128]{0:T(128)S(1)}, s32[128]{0:T(128)}, u32[]{:S(2)}) copy-start(s32[128]{0:T(128)} %param.9) | copy-start | bytes 1540
Sparse Core Ops, SparseCore 0:
  502.6 70.1 reduce-scatter.3
where the time goes:
time: 584 us; the launch traced here: 582 us
  waiting for transfers between devices  403 us (69%)
  local copies, waits for them, and re-layouts  128 us (22%)
  matrix products  19.8 us (3%)
  between operations  14.9 us (3%)
  starting transfers between devices  13.4 us (2%)
    all_to_all x1, waiting for transfers between devices, body(): lax.all_to_all(send_tiles.reshape(n_dev, slots, 2, tile, tile), ('row', '...  356 us
    unnamed x2, waiting for transfers between devices  46.2 us
    unnamed x13, local copies, waits for them, and re-layouts  32.7 us
    another operation x1, local copies, waits for them, and re-layouts, body(): got_tiles.reshape(n_dev * slots, 2 * tile * tile)  25.3 us
    dot_general x1, local copies, waits for them, and re-layouts, body(): jnp.dot(selector, got_tiles.reshape(n_dev * slots, 2 * tile * tile), pref...  22.4 us
    reshape x1, local copies, waits for them, and re-layouts, body(): front.astype(jnp.float32).reshape(2, rows_blocks, tile, cols_blocks, tile)  14.8 us
    slice x3, local copies, waits for them, and re-layouts, body(): stacked = jnp.concatenate([assembled[0], assembled[1]], axis=1)  14 us
    dot_general x1, matrix products, body(): jnp.dot(selector, got_tiles.reshape(n_dev * slots, 2 * tile * tile), pref...  12.9 us
  transfers between devices with their start and end apart: 3, of which 2 were waited for; matrix products, arithmetic and copies ran while one was open for 9% of the time, Pallas kernels for 0%

commit v1 on v0

v1 whole, which is shorter than its diff:
```python
import functools

import jax
import jax.numpy as jnp
from jax import lax
from jax.experimental import pallas as pl
from jax.experimental.pallas import tpu as pltpu
from jax.sharding import PartitionSpec as P

DEPTH = 16


def combine_kernel(
    order, spots, bounds, front, panel, tiles, assembled, partial, acc, held, total, sems
):
    step = pl.program_id(0)
    steps = pl.num_programs(0)
    tile = held.shape[2]
    n_here = acc.shape[0]
    cols_blocks = front.shape[2] // tile
    n_filled = bounds[steps]

    def fetch(e):
        slot = lax.rem(e, DEPTH)
        return pltpu.make_async_copy(tiles.at[order[e]], held.at[slot], sems.at[slot])

    @pl.when(step == 0)
    def _():
        for e in range(DEPTH):
            @pl.when(e < n_filled)
            def _():
                fetch(e).start()

    for b in range(n_here):
        r, c = b // cols_blocks, b % cols_blocks
        acc[b] = front[:, r * tile:(r + 1) * tile, c * tile:(c + 1) * tile].astype(jnp.float32)

    def add(e, carry):
        fetch(e).wait()
        slot = lax.rem(e, DEPTH)
        b = spots[e] - step * n_here
        acc[b] = acc[b] + held[slot].astype(jnp.float32)

        @pl.when(e + DEPTH < n_filled)
        def _():
            fetch(e + DEPTH).start()

        return carry

    lax.fori_loop(bounds[step], bounds[step + 1], add, 0)

    for b in range(n_here):
        r, c = b // cols_blocks, b % cols_blocks
        assembled[:, r * tile:(r + 1) * tile, c * tile:(c + 1) * tile] = acc[b].astype(
            jnp.bfloat16
        )

    @pl.when(step == 0)
    def _():
        total[...] = jnp.zeros_like(total)

    def times(a, b):
        return lax.dot_general(
            a, b, (((0,), (0,)), ((), ())), preferred_element_type=jnp.float32
        )

    total[0] += times(panel[0], assembled[0]) + times(panel[1], assembled[1])
    total[1] += times(panel[0], assembled[1]) - times(panel[1], assembled[0])

    @pl.when(step == steps - 1)
    def _():
        rows_out = partial.shape[2]
        for d in range(partial.shape[0]):
            partial[d] = total[:, d * rows_out:(d + 1) * rows_out, :].astype(jnp.bfloat16)


def combine(front, panel, tiles, order, spots, bounds, n_row, group):
    _, rows, width = front.shape
    p_size = panel.shape[2]
    tile = tiles.shape[2]
    high = group * tile
    steps = rows // high
    return pl.pallas_call(
        combine_kernel,
        grid_spec=pltpu.PrefetchScalarGridSpec(
            num_scalar_prefetch=3,
            grid=(steps,),
            in_specs=[
                pl.BlockSpec((2, high, width), lambda i, *_: (0, i, 0)),
                pl.BlockSpec((2, high, p_size), lambda i, *_: (0, i, 0)),
                pl.BlockSpec(memory_space=pl.ANY),
            ],
            out_specs=[
                pl.BlockSpec((2, high, width), lambda i, *_: (0, i, 0)),
                pl.BlockSpec((n_row, 2, p_size // n_row, width), lambda i, *_: (0, 0, 0, 0)),
            ],
            scratch_shapes=[
                pltpu.VMEM((group * (width // tile), 2, tile, tile), jnp.float32),
                pltpu.VMEM((DEPTH, 2, tile, tile), jnp.bfloat16),
                pltpu.VMEM((2, p_size, width), jnp.float32),
                pltpu.SemaphoreType.DMA((DEPTH,)),
            ],
        ),
        out_shape=[
            jax.ShapeDtypeStruct(front.shape, jnp.bfloat16),
            jax.ShapeDtypeStruct((n_row, 2, p_size // n_row, width), jnp.bfloat16),
        ],
        compiler_params=pltpu.CompilerParams(dimension_semantics=("arbitrary",)),
    )(order, spots, bounds, front, panel, tiles)


def by_spot(got_spots, n_local, per_step):
    n = got_spots.shape[0]
    index = jnp.arange(n, dtype=jnp.int32)
    ahead = (got_spots[None, :] < got_spots[:, None]) | (
        (got_spots[None, :] == got_spots[:, None]) & (index[None, :] < index[:, None])
    )
    place = jnp.sum(ahead.astype(jnp.int32), axis=1)
    at = place[None, :] == index[:, None]
    order = jnp.sum(jnp.where(at, index[None, :], 0), axis=1)
    spots = jnp.sum(jnp.where(at, got_spots[None, :], 0), axis=1)
    edges = jnp.arange(n_local // per_step + 1, dtype=jnp.int32) * per_step
    bounds = jnp.sum((got_spots[None, :] < edges[:, None]).astype(jnp.int32), axis=1)
    return order, spots, bounds


def body(front, child_tiles, tile_owner, tile_spot, tile_count, panel):
    n_row = lax.axis_size("row")
    n_col = lax.axis_size("col")
    n_dev = n_row * n_col
    n_tiles = child_tiles.shape[0]
    tile = child_tiles.shape[2]
    slots = max(2, 2 * n_tiles // n_dev)
    rows_blocks = front.shape[1] // tile
    cols_blocks = front.shape[2] // tile
    n_local = rows_blocks * cols_blocks
    group = 2 if rows_blocks % 2 == 0 else 1
    order = jnp.arange(n_tiles, dtype=jnp.int32)
    owner = tile_owner[:, 0]
    live = order < tile_count[0]
    earlier = (owner[:, None] == owner[None, :]) & live[None, :] & (order[None, :] < order[:, None])
    rank = jnp.sum(earlier.astype(jnp.int32), axis=1)
    slot = jnp.where(live, owner * slots + rank, n_dev * slots)
    here = slot[None, :] == jnp.arange(n_dev * slots, dtype=jnp.int32)[:, None]
    picked = jnp.sum(jnp.where(here, order[None, :], 0), axis=1)
    send_spots = n_local + jnp.sum(jnp.where(here, tile_spot[None, :] - n_local, 0), axis=1)
    send_tiles = child_tiles[picked]
    got_spots = lax.all_to_all(
        send_spots.reshape(n_dev, slots), ("row", "col"), split_axis=0, concat_axis=0, tiled=True
    ).reshape(n_dev * slots)
    got_tiles = lax.all_to_all(
        send_tiles.reshape(n_dev, slots, 2, tile, tile),
        ("row", "col"),
        split_axis=0,
        concat_axis=0,
        tiled=True,
    ).reshape(n_dev * slots, 2, tile, tile)
    listed, spots, bounds = by_spot(got_spots, n_local, group * cols_blocks)
    assembled, partial = combine(
        front, panel, got_tiles, listed, spots, bounds, n_row, group
    )
    parts = lax.all_to_all(partial, "row", split_axis=0, concat_axis=0, tiled=True)
    sample = jnp.sum(parts.astype(jnp.float32), axis=0)
    return (assembled, sample)


def solution(mesh):
    placed = (
        P(None, "row", "col"),
        P(("row", "col"), None, None, None),
        P(("row", "col"), None),
        P(("row", "col")),
        P(("row", "col")),
        P(None, "row", None),
    )
    return jax.shard_map(
        body,
        mesh=mesh,
        in_specs=placed,
        out_specs=(P(None, "row", "col"), P(None, "row", "col")),
        check_vma=False,
    )
```

time: 584 us -> 463 us (0.79)
  local copies, waits for them, and re-layouts: 128 us -> 14 us
  blocking collectives: 0 us -> 42.1 us
  waiting for transfers between devices: 403 us -> 370 us
  matrix products: 19.8 us -> 0 us
  Pallas kernels: 0 us -> 16.5 us
  between operations: 14.9 us -> 1.36 us
    unnamed x2 -> x0, waiting for transfers between devices: 46.2 us -> none
    all_to_all x0 -> x1, blocking collectives: none -> 42.1 us  [body(): lax.all_to_all(partial, 'row', split_axis=0, concat_axis=0, tiled=True)]
    unnamed x13 -> x0, local copies, waits for them, and re-layouts: 32.7 us -> none
    another operation x1 -> x0, local copies, waits for them, and re-layouts: 25.3 us -> none  [body(): got_tiles.reshape(n_dev * slots, 2 * tile * tile)]
    dot_general x1 -> x0, local copies, waits for them, and re-layouts: 22.4 us -> none  [body(): jnp.dot(selector, got_tiles.reshape(n_dev * slots, 2 * tile * tile), pref...]
    dot_general x3 -> x0, matrix products: 19.8 us -> none  [the longest x1 12.9 us: body(): jnp.dot(selector, got_tiles.reshape(n_dev * slots, 2 * tile * tile), pref...]
    pallas_call x0 -> x1, Pallas kernels: none -> 16.5 us  [combine(): pl.pallas_call(combine_kernel, grid_spec=pltpu.PrefetchScalarGridSpec(num...]
    reshape x2 -> x0, local copies, waits for them, and re-layouts: 15.8 us -> none  [the longest x1 14.8 us: body(): front.astype(jnp.float32).reshape(2, rows_blocks, tile, cols_blocks, tile)]
  transfers between devices with their start and end apart: 3 -> 2, of which waited for: 2 -> 1; matrix products, arithmetic and copies ran while one was open for 9% -> 3% of each run, Pallas kernels for 0% -> 0%
where the time goes in v1:
time: 463 us; the launch traced here: 462 us
  waiting for transfers between devices  370 us (80%)
  blocking collectives  42.1 us (9%)
  Pallas kernels  16.5 us (4%)
  local copies, waits for them, and re-layouts  14 us (3%)
  starting transfers between devices  13.4 us (3%)
  other arithmetic  5.06 us (1%)
    all_to_all x1, waiting for transfers between devices, body(): lax.all_to_all(send_tiles.reshape(n_dev, slots, 2, tile, tile), ('row', '...  370 us
    all_to_all x1, blocking collectives, body(): lax.all_to_all(partial, 'row', split_axis=0, concat_axis=0, tiled=True)  42.1 us
    pallas_call x1, Pallas kernels, combine(): pl.pallas_call(combine_kernel, grid_spec=pltpu.PrefetchScalarGridSpec(num...  16.5 us
    gather x1, local copies, waits for them, and re-layouts, body(): send_tiles = child_tiles[picked]  12.7 us
  transfers between devices with their start and end apart: 2, of which 1 were waited for; matrix products, arithmetic and copies ran while one was open for 3% of the time, Pallas kernels for 0%

profile of v1, /device:TPU:0, one launch (start us, length us, event | category | flops | bytes accessed | tf_op | source)
XLA Modules:
  0.0 462.1 jit_solution(9040058902154512457)
XLA Ops:
  1.3 0.9 convert_reduce_fusion.2
  2.2 0.7 add_select_fusion
  2.9 0.2 select_reduce_fusion.2
  3.0 0.7 add.42
  3.7 7.3 %all-to-all-start = ((s32[32,1,8]{2,1,0:T(1,128)}), s32[32,1,8]{2,1,0:T(1,128)S(1)}, u32[]{:S(2)}, u32[]{:S(2)}) async-start(s32[32,1,8]{2,1,0:T(1,128)} %bitcast.2), calls=%async_computation | async-start | bytes 32768 | tf_op jit(solution)/shard_map/all_to_all | solution.py:148
  11.1 12.7 %gather_fusion = bf16[256,2,128,128]{3,2,1,0:T(8,128)(2,1)} fusion(bf16[128,2,128,128]{3,2,1,0:T(8,128)(2,1)} %param.7, s32[1024]{0:T(1024)S(1)} %pad_clamp_fusion), kind=kCustom, calls=%fused_computation | custom fusion | bytes 33555456 | tf_op jit(solution)/shard_map/gather | solution.py:147
  23.8 0.0 all-to-all-done
  23.8 6.0 %all-to-all-start.1 = ((bf16[32,8,2,128,128]{4,3,2,1,0:T(8,128)(2,1)}), bf16[32,8,2,128,128]{4,3,2,1,0:T(8,128)(2,1)}, u32[]{:S(2)}, u32[]{:S(2)}) async-start(bf16[32,8,2,128,128]{4,3,2,1,0:T(8,128)(2,1)} %bitcast.10), calls=%async_computation.1 | async-start | bytes 33554432 | tf_op jit(solution)/shard_map/all_to_all | solution.py:151
  29.9 0.5 broadcast.63
  30.4 0.7 reduce.3
  31.1 0.1 lt.89
  31.2 0.7 convert_reduce_fusion.3.bounds
  31.9 0.2 convert_reduce_fusion.1
  32.1 0.7 select_reduce_fusion
  32.8 369.6 %all-to-all-done.1 = bf16[32,8,2,128,128]{4,3,2,1,0:T(8,128)(2,1)} async-done(((bf16[32,8,2,128,128]{4,3,2,1,0:T(8,128)(2,1)}), bf16[32,8,2,128,128]{4,3,2,1,0:T(8,128)(2,1)}, u32[]{:S(2)}, u32[]{:S(2)}) %all-to-all-start.1) | async-done | bytes 16777248 | tf_op jit(solution)/shard_map/all_to_all | solution.py:151
  402.5 16.5 %shard_map.77 = (bf16[2,2048,768]{2,1,0:T(8,128)(2,1)}, bf16[8,2,64,768]{3,2,1,0:T(8,128)(2,1)}) custom-call(s32[256]{0:T(256)} %get-tuple-element.7.order, s32[256]{0:T(256)} %get-tuple-element.6.spots, s32[9]{0:T(128)} %convert_reduce_fusion.3.bounds, bf16[2,2048,768]{2,1,0:T(8,128)(2,1)} %front.1, bf16[2,2048,512]{2,1,0:T(8,128)(2,1)} %panel.1, ...), custom_call_target="tpu_custom_call" | custom-call | tf_op jit(solution)/shard_map/pallas_call | solution.py:83
  419.0 42.1 %all_to_all.16 = bf16[8,2,64,768]{3,2,1,0:T(8,128)(2,1)S(1)} all-to-all(bf16[8,2,64,768]{3,2,1,0:T(8,128)(2,1)} %get-tuple-element.5), channel_id=1, replica_groups=mesh['row'=8,'col'=4] {'row'}, dimensions={0} | all-to-all | bytes 3145728 | tf_op jit(solution)/shard_map/all_to_all | solution.py:162
  461.1 1.0 convert_reduce_fusion
  (5 shorter events, 0.0 us)
Async XLA Ops:
  3.7 20.1 %all-to-all-start = ((s32[32,1,8]{2,1,0:T(1,128)}), s32[32,1,8]{2,1,0:T(1,128)S(1)}, u32[]{:S(2)}, u32[]{:S(2)}) async-start(s32[32,1,8]{2,1,0:T(1,128)} %bitcast.2), calls=%async_computation | async-start | bytes 32768 | tf_op jit(solution)/shard_map/all_to_all | solution.py:148
  23.8 378.6 %all-to-all-start.1 = ((bf16[32,8,2,128,128]{4,3,2,1,0:T(8,128)(2,1)}), bf16[32,8,2,128,128]{4,3,2,1,0:T(8,128)(2,1)}, u32[]{:S(2)}, u32[]{:S(2)}) async-start(bf16[32,8,2,128,128]{4,3,2,1,0:T(8,128)(2,1)} %bitcast.10), calls=%async_computation.1 | async-start | bytes 33554432 | tf_op jit(solution)/shard_map/all_to_all | solution.py:151

commit v2 on v1

--- a/solution.py
+++ b/solution.py
@@ -11,7 +11,7 @@
 
 
 def combine_kernel(
-    order, spots, bounds, front, panel, tiles, assembled, partial, acc, held, total, sems
+    order, spots, bounds, front, panel, near, far, assembled, partial, acc, held, total, sems
 ):
     step = pl.program_id(0)
     steps = pl.num_programs(0)
@@ -20,30 +20,40 @@
     cols_blocks = front.shape[2] // tile
     n_filled = bounds[steps]
 
+    n_near = near.shape[0]
+
     def fetch(e):
         slot = lax.rem(e, DEPTH)
-        return pltpu.make_async_copy(tiles.at[order[e]], held.at[slot], sems.at[slot])
+        place = order[e]
+
+        @pl.when(place < n_near)
+        def _():
+            pltpu.make_async_copy(near.at[place], held.at[slot], sems.at[slot]).start()
+
+        @pl.when(place >= n_near)
+        def _():
+            pltpu.make_async_copy(far.at[place - n_near], held.at[slot], sems.at[slot]).start()
 
     @pl.when(step == 0)
     def _():
         for e in range(DEPTH):
             @pl.when(e < n_filled)
             def _():
-                fetch(e).start()
+                fetch(e)
 
     for b in range(n_here):
         r, c = b // cols_blocks, b % cols_blocks
         acc[b] = front[:, r * tile:(r + 1) * tile, c * tile:(c + 1) * tile].astype(jnp.float32)
 
     def add(e, carry):
-        fetch(e).wait()
         slot = lax.rem(e, DEPTH)
+        pltpu.make_async_copy(near.at[0], held.at[slot], sems.at[slot]).wait()
         b = spots[e] - step * n_here
         acc[b] = acc[b] + held[slot].astype(jnp.float32)
 
         @pl.when(e + DEPTH < n_filled)
         def _():
-            fetch(e + DEPTH).start()
+            fetch(e + DEPTH)
 
         return carry
 
@@ -74,10 +84,10 @@
             partial[d] = total[:, d * rows_out:(d + 1) * rows_out, :].astype(jnp.bfloat16)
 
 
-def combine(front, panel, tiles, order, spots, bounds, n_row, group):
+def combine(front, panel, near, far, order, spots, bounds, n_row, group):
     _, rows, width = front.shape
     p_size = panel.shape[2]
-    tile = tiles.shape[2]
+    tile = near.shape[2]
     high = group * tile
     steps = rows // high
     return pl.pallas_call(
@@ -88,6 +98,7 @@
             in_specs=[
                 pl.BlockSpec((2, high, width), lambda i, *_: (0, i, 0)),
                 pl.BlockSpec((2, high, p_size), lambda i, *_: (0, i, 0)),
+                pl.BlockSpec(memory_space=pl.ANY),
                 pl.BlockSpec(memory_space=pl.ANY),
             ],
             out_specs=[
@@ -106,7 +117,7 @@
             jax.ShapeDtypeStruct((n_row, 2, p_size // n_row, width), jnp.bfloat16),
         ],
         compiler_params=pltpu.CompilerParams(dimension_semantics=("arbitrary",)),
-    )(order, spots, bounds, front, panel, tiles)
+    )(order, spots, bounds, front, panel, near, far)
 
 
 def by_spot(got_spots, n_local, per_step):
@@ -124,40 +135,156 @@
     return order, spots, bounds
 
 
+def swap_kernel(n_half, n_col, slots, length, *refs):
+    if length:
+        send, got, mirrored, send_sems, recv_sems = refs
+    else:
+        send, got, send_sems, recv_sems = refs
+    row, col = lax.axis_index("row"), lax.axis_index("col")
+    half_rows = n_half // n_col
+    half = row // half_rows
+    k = lax.rem(row, half_rows) * n_col + col
+
+    def peer(j):
+        return lax.rem(k + j, n_half)
+
+    def device(p):
+        return (half * half_rows + p // n_col, lax.rem(p, n_col))
+
+    across = (lax.rem(row + half_rows, 2 * half_rows), col)
+    mesh_id = pl.DeviceIdType.MESH
+    barrier = pltpu.get_barrier_semaphore()
+    for j in range(1, n_half):
+        pl.semaphore_signal(barrier, inc=1, device_id=device(peer(j)), device_id_type=mesh_id)
+    if length:
+        pl.semaphore_signal(barrier, inc=1, device_id=across, device_id_type=mesh_id)
+    pl.semaphore_wait(barrier, n_half if length else n_half - 1)
+
+    copies = []
+    if length:
+        copies.append(
+            pltpu.make_async_remote_copy(
+                src_ref=send.at[pl.ds(n_half * slots, length)],
+                dst_ref=mirrored.at[pl.ds(0, length)],
+                send_sem=send_sems.at[0],
+                recv_sem=recv_sems.at[0],
+                device_id=across,
+                device_id_type=mesh_id,
+            )
+        )
+    for j in range(1, n_half):
+        copies.append(
+            pltpu.make_async_remote_copy(
+                src_ref=send.at[pl.ds(peer(j) * slots, slots)],
+                dst_ref=got.at[pl.ds(k * slots, slots)],
+                send_sem=send_sems.at[j],
+                recv_sem=recv_sems.at[j],
+                device_id=device(peer(j)),
+                device_id_type=mesh_id,
+            )
+        )
+    for copy in copies:
+        copy.start()
+    own = pltpu.make_async_copy(
+        send.at[pl.ds(k * slots, slots)], got.at[pl.ds(k * slots, slots)], send_sems.at[n_half]
+    )
+    own.start()
+    own.wait()
+    for copy in copies:
+        copy.wait()
+
+
+def swap(send, n_half, n_col, slots, length, number):
+    shape = jax.ShapeDtypeStruct((n_half * slots,) + send.shape[1:], send.dtype)
+    count = 2 if length else 1
+    return pl.pallas_call(
+        functools.partial(swap_kernel, n_half, n_col, slots, length),
+        in_specs=[pl.BlockSpec(memory_space=pl.ANY)],
+        out_specs=[pl.BlockSpec(memory_space=pl.ANY)] * count,
+        out_shape=[shape] * count,
+        scratch_shapes=[
+            pltpu.SemaphoreType.DMA((n_half + 1,)),
+            pltpu.SemaphoreType.DMA((n_half,)),
+        ],
+        compiler_params=pltpu.CompilerParams(collective_id=number, has_side_effects=True),
+    )(send)
+
+
 def body(front, child_tiles, tile_owner, tile_spot, tile_count, panel):
     n_row = lax.axis_size("row")
     n_col = lax.axis_size("col")
     n_dev = n_row * n_col
+    n_half = n_dev // 2
     n_tiles = child_tiles.shape[0]
     tile = child_tiles.shape[2]
     slots = max(2, 2 * n_tiles // n_dev)
+    room = n_half * slots
     rows_blocks = front.shape[1] // tile
     cols_blocks = front.shape[2] // tile
     n_local = rows_blocks * cols_blocks
     group = 2 if rows_blocks % 2 == 0 else 1
+    half = lax.axis_index("row") // (n_row // 2)
+    mine = lax.rem(lax.axis_index("row"), n_row // 2) * n_col + lax.axis_index("col")
     order = jnp.arange(n_tiles, dtype=jnp.int32)
+    devices = jnp.arange(n_dev, dtype=jnp.int32)
+    places = jnp.arange(n_half, dtype=jnp.int32)
+    rows = jnp.arange(2 * room, dtype=jnp.int32)
     owner = tile_owner[:, 0]
     live = order < tile_count[0]
+    is_far = live & (owner // n_half != half)
     earlier = (owner[:, None] == owner[None, :]) & live[None, :] & (order[None, :] < order[:, None])
     rank = jnp.sum(earlier.astype(jnp.int32), axis=1)
-    slot = jnp.where(live, owner * slots + rank, n_dev * slots)
-    here = slot[None, :] == jnp.arange(n_dev * slots, dtype=jnp.int32)[:, None]
-    picked = jnp.sum(jnp.where(here, order[None, :], 0), axis=1)
-    send_spots = n_local + jnp.sum(jnp.where(here, tile_spot[None, :] - n_local, 0), axis=1)
-    send_tiles = child_tiles[picked]
-    got_spots = lax.all_to_all(
-        send_spots.reshape(n_dev, slots), ("row", "col"), split_axis=0, concat_axis=0, tiled=True
-    ).reshape(n_dev * slots)
-    got_tiles = lax.all_to_all(
-        send_tiles.reshape(n_dev, slots, 2, tile, tile),
-        ("row", "col"),
-        split_axis=0,
-        concat_axis=0,
-        tiled=True,
-    ).reshape(n_dev * slots, 2, tile, tile)
+    below = jnp.sum(
+        (is_far[None, :] & (owner[None, :] < owner[:, None])).astype(jnp.int32), axis=1
+    )
+    spread = jnp.where(live, owner * slots + rank, 2 * room)
+    packed = jnp.where(
+        is_far, room + below + rank, lax.rem(owner, n_half) * slots + rank
+    )
+    packed = jnp.where(live, packed, 2 * room)
+    picked = jnp.sum(jnp.where(packed[None, :] == rows[:, None], order[None, :], 0), axis=1)
+    send_spots = n_local + jnp.sum(
+        jnp.where(spread[None, :] == rows[:, None], tile_spot[None, :] - n_local, 0), axis=1
+    )
+    far_owner = jnp.where(is_far, lax.rem(owner, n_half), n_half)
+    far_counts = jnp.sum((far_owner[None, :] == places[:, None]).astype(jnp.int32), axis=1)
+    news = jnp.concatenate(
+        [
+            send_spots.reshape(n_dev, slots),
+            jnp.broadcast_to(far_counts[None, :], (n_dev, n_half)),
+        ],
+        axis=1,
+    )
+    heard = lax.all_to_all(news, ("row", "col"), split_axis=0, concat_axis=0, tiled=True)
+    send = child_tiles[picked]
+    fullest = jnp.max(jnp.sum(heard[:, slots:], axis=1))
+    levels = sorted({-(-room * part // 16) for part in (9, 10, 16)})
+    level = sum((fullest > size).astype(jnp.int32) for size in levels[:-1])
+    near, mirrored = lax.switch(
+        level,
+        [
+            functools.partial(
+                lambda size, number, s: tuple(swap(s, n_half, n_col, slots, size, number)),
+                size,
+                number,
+            )
+            for number, size in enumerate(levels)
+        ],
+        send,
+    )
+    across = (1 - half) * n_half + mine
+    theirs = jnp.sum(
+        jnp.where(devices[:, None] == across, heard[:, slots:], 0), axis=0
+    )
+    start = jnp.sum(jnp.where(places[None, :] < places[:, None], theirs[None, :], 0), axis=1)
+    ranks = jnp.arange(slots, dtype=jnp.int32)
+    taken = jnp.where(ranks[None, :] < theirs[:, None], start[:, None] + ranks[None, :], 0)
+    (far,) = swap(mirrored[taken.reshape(room)], n_half, n_col, slots, 0, len(levels))
+    spots_in = heard[:, :slots].reshape(2, room)
+    got_spots = jnp.where(half == 0, spots_in, spots_in[::-1]).reshape(2 * room)
     listed, spots, bounds = by_spot(got_spots, n_local, group * cols_blocks)
     assembled, partial = combine(
-        front, panel, got_tiles, listed, spots, bounds, n_row, group
+        front, panel, near, far, listed, spots, bounds, n_row, group
     )
     parts = lax.all_to_all(partial, "row", split_axis=0, concat_axis=0, tiled=True)
     sample = jnp.sum(parts.astype(jnp.float32), axis=0)

time: 463 us -> 480 us (1.037)
  Pallas kernels: 16.5 us -> 395 us
  waiting for transfers between devices: 370 us -> 0.01 us
  local copies, waits for them, and re-layouts: 14 us -> 23.2 us
  starting transfers between devices: 13.4 us -> 7.33 us
    all_to_all x2 -> x1, waiting for transfers between devices: 370 us -> 0.01 us  [body(): lax.all_to_all(news, ('row', 'col'), split_axis=0, concat_axis=0, tiled=T...]
    pallas_call x0 -> x2, Pallas kernels: none -> 369 us  [swap(): pl.pallas_call(functools.partial(swap_kernel, n_half, n_col, slots, lengt...]
    pallas_call x1, Pallas kernels: 16.5 us -> 26.8 us  [combine(): pl.pallas_call(combine_kernel, grid_spec=pltpu.PrefetchScalarGridSpec(num...]
    gather x1 -> x2, local copies, waits for them, and re-layouts: 12.7 us -> 22.8 us  [the longest x1 13 us: body(): send = child_tiles[picked]]
    all_to_all x2 -> x1, starting transfers between devices: 13.4 us -> 7.33 us  [body(): lax.all_to_all(news, ('row', 'col'), split_axis=0, concat_axis=0, tiled=T...]
  transfers between devices with their start and end apart: 2 -> 1, of which waited for: 1 -> 0; matrix products, arithmetic and copies ran while one was open for 3% -> 3% of each run, Pallas kernels for 0% -> 0%
where the time goes in v2:
time: 480 us
  Pallas kernels  395 us (82%)
  blocking collectives  44.3 us (9%)
  local copies, waits for them, and re-layouts  23.2 us (5%)
  other arithmetic  7.47 us (2%)
  starting transfers between devices  7.33 us (2%)
    pallas_call x2, Pallas kernels, swap(): pl.pallas_call(functools.partial(swap_kernel, n_half, n_col, slots, lengt...  369 us
    all_to_all x1, blocking collectives, body(): lax.all_to_all(partial, 'row', split_axis=0, concat_axis=0, tiled=True)  44.3 us
    pallas_call x1, Pallas kernels, combine(): pl.pallas_call(combine_kernel, grid_spec=pltpu.PrefetchScalarGridSpec(num...  26.8 us
    gather x1, local copies, waits for them, and re-layouts, body(): send = child_tiles[picked]  13 us
    gather x1, local copies, waits for them, and re-layouts, body(): mirrored[taken.reshape(room)]  9.84 us
  transfers between devices with their start and end apart: 1, of which 0 were waited for; matrix products, arithmetic and copies ran while one was open for 3% of the time, Pallas kernels for 0%

profile of v2, /device:TPU:0, one launch (start us, length us, event | category | flops | bytes accessed | tf_op | source)
XLA Modules:
  0.0 480.4 jit_solution(7132130652542483674)
XLA Ops:
  1.3 0.7 broadcast_add_fusion.1
  2.0 0.7 broadcast_select_fusion
  2.6 0.9 convert_reduce_fusion.2
  3.5 0.7 select_select_fusion
  4.2 0.2 select_reduce_fusion.2
  4.4 0.1 add.107
  4.5 0.1 convert_reduce_fusion.5
  4.6 0.1 pad.1.clone
  4.6 0.6 pad_add_fusion
  5.3 7.3 %all-to-all-start = ((s32[32,1,24]{2,1,0:T(1,128)}), s32[32,1,24]{2,1,0:T(1,128)S(1)}, u32[]{:S(2)}, u32[]{:S(2)}) async-start(s32[32,1,24]{2,1,0:T(1,128)} %bitcast.2), calls=%async_computation | async-start | bytes 32768 | tf_op jit(solution)/shard_map/all_to_all | solution.py:258
  12.7 13.0 %gather_fusion = bf16[256,2,128,128]{3,2,1,0:T(8,128)(2,1)} fusion(bf16[128,2,128,128]{3,2,1,0:T(8,128)(2,1)} %param.10, s32[1024]{0:T(1024)S(1)} %pad_clamp_fusion.1), kind=kCustom, calls=%fused_computation | custom fusion | bytes 33555456 | tf_op jit(solution)/shard_map/gather | solution.py:259
  25.6 0.0 all-to-all-done
  25.6 0.1 reshape.180
  25.8 0.2 convert_reduce_fusion.1
  25.9 0.7 select_reduce_fusion
  26.7 0.7 convert_reduce_fusion.4.bounds
  27.4 0.2 select_reduce_fusion.4
  27.6 0.6 reduce_max.9
  29.5 0.1 select_reduce_fusion.5
  29.6 0.1 add_select_fusion
  29.7 0.1 select_n.130
  29.8 232.9 %conditional.1 = ((bf16[128,2,128,128]{3,2,1,0:T(8,128)(2,1)}, bf16[128,2,128,128]{3,2,1,0:T(8,128)(2,1)})) conditional(s32[]{:T(128)} %clamp.3, bf16[256,2,128,128]{3,2,1,0:T(8,128)(2,1)} %gather_fusion, bf16[256,2,128,128]{3,2,1,0:T(8,128)(2,1)} %gather_fusion, bf16[256,2,128,128]{3,2,1,0:T(8,128)(2,1)} %gather_fusion), branch_computations={%region_11.12_spmd, %region_12.13_spmd, %region_13.14_spmd} | conditional | bytes 8 | solution.py:263
  29.9 232.8 %branch_0_fun.1 = (bf16[128,2,128,128]{3,2,1,0:T(8,128)(2,1)}, bf16[128,2,128,128]{3,2,1,0:T(8,128)(2,1)}) custom-call(bf16[256,2,128,128]{3,2,1,0:T(8,128)(2,1)} %refs_0_), custom_call_target="tpu_custom_call" | custom-call | tf_op jit(solution)/shard_map/cond/branch_0_fun/pallas_call | solution.py:200
  262.7 9.8 %gather_fusion.1 = bf16[128,2,128,128]{3,2,1,0:T(8,128)(2,1)} fusion(bf16[128,2,128,128]{3,2,1,0:T(8,128)(2,1)} %get-tuple-element.10, s32[1024]{0:T(1024)S(1)} %pad_clamp_fusion), kind=kCustom, calls=%fused_computation.1 | custom fusion | bytes 16777728 | tf_op jit(solution)/shard_map/gather | solution.py:282
  272.6 135.8 %shard_map.77.far = bf16[128,2,128,128]{3,2,1,0:T(8,128)(2,1)} custom-call(bf16[128,2,128,128]{3,2,1,0:T(8,128)(2,1)} %gather_fusion.1), custom_call_target="tpu_custom_call" | custom-call | tf_op jit(solution)/shard_map/pallas_call | solution.py:200
  408.4 26.8 %shard_map.78 = (bf16[2,2048,768]{2,1,0:T(8,128)(2,1)}, bf16[8,2,64,768]{3,2,1,0:T(8,128)(2,1)}) custom-call(s32[256]{0:T(256)} %get-tuple-element.16.order, s32[256]{0:T(256)} %get-tuple-element.15.spots, s32[9]{0:T(128)} %convert_reduce_fusion.4.bounds, bf16[2,2048,768]{2,1,0:T(8,128)(2,1)} %front.1, bf16[2,2048,512]{2,1,0:T(8,128)(2,1)} %panel.1, ...), custom_call_target="tpu_custom_call" | custom-call | tf_op jit(solution)/shard_map/pallas_call | solution.py:93
  435.2 44.3 %all_to_all.17 = bf16[8,2,64,768]{3,2,1,0:T(8,128)(2,1)S(1)} all-to-all(bf16[8,2,64,768]{3,2,1,0:T(8,128)(2,1)} %get-tuple-element.12), channel_id=1, replica_groups=mesh['row'=8,'col'=4] {'row'}, dimensions={0} | all-to-all | bytes 3145728 | tf_op jit(solution)/shard_map/all_to_all | solution.py:289
  479.5 1.0 convert_reduce_fusion
  (10 shorter events, 0.1 us)
Async XLA Ops:
  5.3 20.4 %all-to-all-start = ((s32[32,1,24]{2,1,0:T(1,128)}), s32[32,1,24]{2,1,0:T(1,128)S(1)}, u32[]{:S(2)}, u32[]{:S(2)}) async-start(s32[32,1,24]{2,1,0:T(1,128)} %bitcast.2), calls=%async_computation | async-start | bytes 32768 | tf_op jit(solution)/shard_map/all_to_all | solution.py:258

commit v3 on v2

--- a/solution.py
+++ b/solution.py
@@ -11,7 +11,7 @@
 
 
 def combine_kernel(
-    order, spots, bounds, front, panel, near, far, assembled, partial, acc, held, total, sems
+    order, spots, bounds, front, panel, near, crossed, passed, assembled, partial, acc, held, total, sems
 ):
     step = pl.program_id(0)
     steps = pl.num_programs(0)
@@ -20,19 +20,20 @@
     cols_blocks = front.shape[2] // tile
     n_filled = bounds[steps]
 
-    n_near = near.shape[0]
+    sources, first = [], 0
+    for source in (near, crossed, passed):
+        sources.append((source, first))
+        first += source.shape[0]
 
     def fetch(e):
         slot = lax.rem(e, DEPTH)
         place = order[e]
-
-        @pl.when(place < n_near)
-        def _():
-            pltpu.make_async_copy(near.at[place], held.at[slot], sems.at[slot]).start()
-
-        @pl.when(place >= n_near)
-        def _():
-            pltpu.make_async_copy(far.at[place - n_near], held.at[slot], sems.at[slot]).start()
+        for source, first in sources:
+            @pl.when((place >= first) & (place < first + source.shape[0]))
+            def _():
+                pltpu.make_async_copy(
+                    source.at[place - first], held.at[slot], sems.at[slot]
+                ).start()
 
     @pl.when(step == 0)
     def _():
@@ -84,7 +85,7 @@
             partial[d] = total[:, d * rows_out:(d + 1) * rows_out, :].astype(jnp.bfloat16)
 
 
-def combine(front, panel, near, far, order, spots, bounds, n_row, group):
+def combine(front, panel, near, crossed, passed, order, spots, bounds, n_row, group):
     _, rows, width = front.shape
     p_size = panel.shape[2]
     tile = near.shape[2]
@@ -98,6 +99,7 @@
             in_specs=[
                 pl.BlockSpec((2, high, width), lambda i, *_: (0, i, 0)),
                 pl.BlockSpec((2, high, p_size), lambda i, *_: (0, i, 0)),
+                pl.BlockSpec(memory_space=pl.ANY),
                 pl.BlockSpec(memory_space=pl.ANY),
                 pl.BlockSpec(memory_space=pl.ANY),
             ],
@@ -117,7 +119,7 @@
             jax.ShapeDtypeStruct((n_row, 2, p_size // n_row, width), jnp.bfloat16),
         ],
         compiler_params=pltpu.CompilerParams(dimension_semantics=("arbitrary",)),
-    )(order, spots, bounds, front, panel, near, far)
+    )(order, spots, bounds, front, panel, near, crossed, passed)
 
 
 def by_spot(got_spots, n_local, per_step):
@@ -135,58 +137,89 @@
     return order, spots, bounds
 
 
-def swap_kernel(n_half, n_col, slots, length, *refs):
+def peers_in_turn(n):
+    return sorted(range(1, n), key=lambda j: (bin(j).count("1"), -j))
+
+
+def swap_kernel(n_half, n_col, slots, direct, length, *refs):
     if length:
-        send, got, mirrored, send_sems, recv_sems = refs
+        send, got, crossed, mirrored, send_sems, recv_sems = refs
     else:
         send, got, send_sems, recv_sems = refs
     row, col = lax.axis_index("row"), lax.axis_index("col")
     half_rows = n_half // n_col
     half = row // half_rows
     k = lax.rem(row, half_rows) * n_col + col
+    even = n_half & (n_half - 1) == 0
 
     def peer(j):
-        return lax.rem(k + j, n_half)
-
-    def device(p):
-        return (half * half_rows + p // n_col, lax.rem(p, n_col))
-
-    across = (lax.rem(row + half_rows, 2 * half_rows), col)
+        if not even:
+            return lax.rem(k + j, n_half)
+        place = k
+        for b in range(n_half.bit_length() - 1):
+            if j >> b & 1:
+                place = place + (1 << b) * (1 - 2 * ((k // (1 << b)) % 2))
+        return place
+
+    def device(side, p):
+        return (side * half_rows + p // n_col, lax.rem(p, n_col))
+
     mesh_id = pl.DeviceIdType.MESH
     barrier = pltpu.get_barrier_semaphore()
     for j in range(1, n_half):
-        pl.semaphore_signal(barrier, inc=1, device_id=device(peer(j)), device_id_type=mesh_id)
+        pl.semaphore_signal(
+            barrier, inc=1, device_id=device(half, peer(j)), device_id_type=mesh_id
+        )
     if length:
-        pl.semaphore_signal(barrier, inc=1, device_id=across, device_id_type=mesh_id)
-    pl.semaphore_wait(barrier, n_half if length else n_half - 1)
+        for j in range(n_half):
+            pl.semaphore_signal(
+                barrier, inc=1, device_id=device(1 - half, peer(j)), device_id_type=mesh_id
+            )
+    pl.semaphore_wait(barrier, 2 * n_half - 1 if length else n_half - 1)
 
     copies = []
-    if length:
+
+    def post(source, target, number, to):
         copies.append(
             pltpu.make_async_remote_copy(
-                src_ref=send.at[pl.ds(n_half * slots, length)],
-                dst_ref=mirrored.at[pl.ds(0, length)],
-                send_sem=send_sems.at[0],
-                recv_sem=recv_sems.at[0],
-                device_id=across,
+                src_ref=source,
+                dst_ref=target,
+                send_sem=send_sems.at[number],
+                recv_sem=recv_sems.at[number],
+                device_id=to,
                 device_id_type=mesh_id,
             )
         )
-    for j in range(1, n_half):
-        copies.append(
-            pltpu.make_async_remote_copy(
-                src_ref=send.at[pl.ds(peer(j) * slots, slots)],
-                dst_ref=got.at[pl.ds(k * slots, slots)],
-                send_sem=send_sems.at[j],
-                recv_sem=recv_sems.at[j],
-                device_id=device(peer(j)),
-                device_id_type=mesh_id,
+
+    turn = peers_in_turn(n_half)
+    if length:
+        base = n_half * slots
+        post(
+            send.at[pl.ds(base + n_half * direct, length)],
+            mirrored.at[pl.ds(0, length)],
+            0,
+            device(1 - half, k),
+        )
+        for j in [0] + turn:
+            post(
+                send.at[pl.ds(base + peer(j) * direct, direct)],
+                crossed.at[pl.ds(k * direct, direct)],
+                n_half + j,
+                device(1 - half, peer(j)),
             )
+    for j in turn:
+        post(
+            send.at[pl.ds(peer(j) * slots, slots)],
+            got.at[pl.ds(k * slots, slots)],
+            j,
+            device(half, peer(j)),
         )
     for copy in copies:
         copy.start()
     own = pltpu.make_async_copy(
-        send.at[pl.ds(k * slots, slots)], got.at[pl.ds(k * slots, slots)], send_sems.at[n_half]
+        send.at[pl.ds(k * slots, slots)],
+        got.at[pl.ds(k * slots, slots)],
+        send_sems.at[2 * n_half],
     )
     own.start()
     own.wait()
@@ -194,20 +227,107 @@
         copy.wait()
 
 
-def swap(send, n_half, n_col, slots, length, number):
-    shape = jax.ShapeDtypeStruct((n_half * slots,) + send.shape[1:], send.dtype)
-    count = 2 if length else 1
+def swap(send, n_half, n_col, slots, direct, room, length, number):
+    def shape(rows):
+        return jax.ShapeDtypeStruct((rows,) + send.shape[1:], send.dtype)
+
+    shapes = [shape(n_half * slots)]
+    if length:
+        shapes += [shape(n_half * direct), shape(room)]
     return pl.pallas_call(
-        functools.partial(swap_kernel, n_half, n_col, slots, length),
+        functools.partial(swap_kernel, n_half, n_col, slots, direct, length),
         in_specs=[pl.BlockSpec(memory_space=pl.ANY)],
-        out_specs=[pl.BlockSpec(memory_space=pl.ANY)] * count,
-        out_shape=[shape] * count,
+        out_specs=[pl.BlockSpec(memory_space=pl.ANY)] * len(shapes),
+        out_shape=shapes,
         scratch_shapes=[
-            pltpu.SemaphoreType.DMA((n_half + 1,)),
-            pltpu.SemaphoreType.DMA((n_half,)),
+            pltpu.SemaphoreType.DMA((2 * n_half + 1,)),
+            pltpu.SemaphoreType.DMA((2 * n_half,)),
         ],
         compiler_params=pltpu.CompilerParams(collective_id=number, has_side_effects=True),
     )(send)
+
+
+def fold_kernel(n_row, part, out, sums, landed, send_sems, recv_sems):
+    row, col = lax.axis_index("row"), lax.axis_index("col")
+    bits = n_row.bit_length() - 1
+    width = part.shape[3]
+
+    def flip(t):
+        place = row
+        for b in range(bits):
+            if t >> b & 1:
+                place = place + (1 << b) * (1 - 2 * ((row // (1 << b)) % 2))
+        return place
+
+    mesh_id = pl.DeviceIdType.MESH
+    barrier = pltpu.get_barrier_semaphore()
+    for b in range(bits):
+        pl.semaphore_signal(
+            barrier, inc=1, device_id=(flip(1 << b), col), device_id_type=mesh_id
+        )
+    pl.semaphore_wait(barrier, bits)
+
+    orders = [list(range(bits))]
+    if width % 256 == 0 and bits > 1:
+        orders.append([1, 0] + list(range(2, bits)))
+    span = width // len(orders)
+    left = [list(range(n_row)) for _ in orders]
+    parts_of = [{t: [] for t in range(n_row)} for _ in orders]
+    used = 0
+
+    def value(h, t):
+        total = part[flip(t), :, :, h * span:(h + 1) * span].astype(jnp.float32)
+        for slot in parts_of[h][t]:
+            total = total + landed[slot].astype(jnp.float32)
+        return total
+
+    for step in range(bits):
+        copies = []
+        for h, order in enumerate(orders):
+            bit = 1 << order[step]
+            for t in [t for t in left[h] if t & bit]:
+                if step == 0:
+                    source = part.at[flip(t), :, :, pl.ds(h * span, span)]
+                else:
+                    sums[used] = value(h, t).astype(jnp.bfloat16)
+                    source = sums.at[used]
+                copy = pltpu.make_async_remote_copy(
+                    src_ref=source,
+                    dst_ref=landed.at[used],
+                    send_sem=send_sems.at[used],
+                    recv_sem=recv_sems.at[used],
+                    device_id=(flip(bit), col),
+                    device_id_type=mesh_id,
+                )
+                copy.start()
+                copies.append((copy, h, t ^ bit, used))
+                used += 1
+            left[h] = [t for t in left[h] if not t & bit]
+        for copy, h, t, slot in copies:
+            copy.wait()
+            parts_of[h][t].append(slot)
+    for h in range(len(orders)):
+        out[:, :, h * span:(h + 1) * span] = value(h, 0)
+
+
+def fold(partial, n_row, number):
+    _, _, rows_out, width = partial.shape
+    halves = 2 if width % 256 == 0 and n_row > 2 else 1
+    count = halves * (n_row - 1)
+    block = (count, 2, rows_out, width // halves)
+    return pl.pallas_call(
+        functools.partial(fold_kernel, n_row),
+        in_specs=[pl.BlockSpec(memory_space=pltpu.VMEM)],
+        out_specs=pl.BlockSpec(memory_space=pltpu.VMEM),
+        out_shape=jax.ShapeDtypeStruct((2, rows_out, width), jnp.float32),
+        scratch_shapes=[
+            pltpu.VMEM(block, jnp.bfloat16),
+            pltpu.VMEM(block, jnp.bfloat16),
+            pltpu.SemaphoreType.DMA((count,)),
+            pltpu.SemaphoreType.DMA((count,)),
+        ],
+        compiler_params=pltpu.CompilerParams(collective_id=number, has_side_effects=True),
+    )(partial)
 
 
 def body(front, child_tiles, tile_owner, tile_spot, tile_count, panel):
@@ -218,7 +338,11 @@
     n_tiles = child_tiles.shape[0]
     tile = child_tiles.shape[2]
     slots = max(2, 2 * n_tiles // n_dev)
-    room = n_half * slots
+    direct = slots // 2
+    beyond = slots - direct
+    room = n_half * beyond
+    near_rows = n_half * slots
+    far_rows = n_half * direct
     rows_blocks = front.shape[1] // tile
     cols_blocks = front.shape[2] // tile
     n_local = rows_blocks * cols_blocks
@@ -228,25 +352,29 @@
     order = jnp.arange(n_tiles, dtype=jnp.int32)
     devices = jnp.arange(n_dev, dtype=jnp.int32)
     places = jnp.arange(n_half, dtype=jnp.int32)
-    rows = jnp.arange(2 * room, dtype=jnp.int32)
+    rows = jnp.arange(2 * near_rows, dtype=jnp.int32)
     owner = tile_owner[:, 0]
     live = order < tile_count[0]
     is_far = live & (owner // n_half != half)
     earlier = (owner[:, None] == owner[None, :]) & live[None, :] & (order[None, :] < order[:, None])
     rank = jnp.sum(earlier.astype(jnp.int32), axis=1)
+    is_over = is_far & (rank >= direct)
     below = jnp.sum(
-        (is_far[None, :] & (owner[None, :] < owner[:, None])).astype(jnp.int32), axis=1
-    )
-    spread = jnp.where(live, owner * slots + rank, 2 * room)
+        (is_over[None, :] & (owner[None, :] < owner[:, None])).astype(jnp.int32), axis=1
+    )
+    spread = jnp.where(live, owner * slots + rank, 2 * near_rows)
+    place = lax.rem(owner, n_half)
     packed = jnp.where(
-        is_far, room + below + rank, lax.rem(owner, n_half) * slots + rank
-    )
-    packed = jnp.where(live, packed, 2 * room)
+        is_over,
+        near_rows + far_rows + below + rank - direct,
+        jnp.where(is_far, near_rows + place * direct + rank, place * slots + rank),
+    )
+    packed = jnp.where(live, packed, 2 * near_rows)
     picked = jnp.sum(jnp.where(packed[None, :] == rows[:, None], order[None, :], 0), axis=1)
     send_spots = n_local + jnp.sum(
         jnp.where(spread[None, :] == rows[:, None], tile_spot[None, :] - n_local, 0), axis=1
     )
-    far_owner = jnp.where(is_far, lax.rem(owner, n_half), n_half)
+    far_owner = jnp.where(is_over, place, n_half)
     far_counts = jnp.sum((far_owner[None, :] == places[:, None]).astype(jnp.int32), axis=1)
     news = jnp.concatenate(
         [
@@ -258,13 +386,15 @@
     heard = lax.all_to_all(news, ("row", "col"), split_axis=0, concat_axis=0, tiled=True)
     send = child_tiles[picked]
     fullest = jnp.max(jnp.sum(heard[:, slots:], axis=1))
-    levels = sorted({-(-room * part // 16) for part in (9, 10, 16)})
+    levels = sorted({-(-room * part // 16) for part in (4, 5, 6, 8, 16)})
     level = sum((fullest > size).astype(jnp.int32) for size in levels[:-1])
-    near, mirrored = lax.switch(
+    near, crossed, mirrored = lax.switch(
         level,
         [
             functools.partial(
-                lambda size, number, s: tuple(swap(s, n_half, n_col, slots, size, number)),
+                lambda size, number, s: tuple(
+                    swap(s, n_half, n_col, slots, direct, room, size, number)
+                ),
                 size,
                 number,
             )
@@ -277,17 +407,26 @@
         jnp.where(devices[:, None] == across, heard[:, slots:], 0), axis=0
     )
     start = jnp.sum(jnp.where(places[None, :] < places[:, None], theirs[None, :], 0), axis=1)
-    ranks = jnp.arange(slots, dtype=jnp.int32)
+    ranks = jnp.arange(beyond, dtype=jnp.int32)
     taken = jnp.where(ranks[None, :] < theirs[:, None], start[:, None] + ranks[None, :], 0)
-    (far,) = swap(mirrored[taken.reshape(room)], n_half, n_col, slots, 0, len(levels))
-    spots_in = heard[:, :slots].reshape(2, room)
-    got_spots = jnp.where(half == 0, spots_in, spots_in[::-1]).reshape(2 * room)
+    (passed,) = swap(
+        mirrored[taken.reshape(room)], n_half, n_col, beyond, direct, room, 0, len(levels)
+    )
+    spots_in = heard[:, :slots].reshape(2, n_half, slots)
+    spots_near = jnp.where(half == 0, spots_in[0], spots_in[1])
+    spots_far = jnp.where(half == 0, spots_in[1], spots_in[0])
+    got_spots = jnp.concatenate(
+        [
+            spots_near.reshape(near_rows),
+            spots_far[:, :direct].reshape(far_rows),
+            spots_far[:, direct:].reshape(room),
+        ]
+    )
     listed, spots, bounds = by_spot(got_spots, n_local, group * cols_blocks)
     assembled, partial = combine(
-        front, panel, near, far, listed, spots, bounds, n_row, group
-    )
-    parts = lax.all_to_all(partial, "row", split_axis=0, concat_axis=0, tiled=True)
-    sample = jnp.sum(parts.astype(jnp.float32), axis=0)
+        front, panel, near, crossed, passed, listed, spots, bounds, n_row, group
+    )
+    sample = fold(partial, n_row, len(levels) + 1)
     return (assembled, sample)
 
 

time: 480 us -> 407 us (0.85)
  blocking collectives: 44.3 us -> 0 us
  Pallas kernels: 395 us -> 368 us
    all_to_all x1 -> x0, blocking collectives: 44.3 us -> none  [body(): lax.all_to_all(partial, 'row', split_axis=0, concat_axis=0, tiled=True)]
    pallas_call x2 -> x3, Pallas kernels: 369 us -> 351 us  [the longest x2 311 us: swap(): pl.pallas_call(functools.partial(swap_kernel, n_half, n_col, slots, direc...]
    pallas_call x1, Pallas kernels: 26.8 us -> 17 us  [combine(): pl.pallas_call(combine_kernel, grid_spec=pltpu.PrefetchScalarGridSpec(num...]
where the time goes in v3:
time: 407 us; the launch traced here: 408 us
  Pallas kernels  368 us (90%)
  local copies, waits for them, and re-layouts  20.4 us (5%)
  other arithmetic  7.49 us (2%)
  starting transfers between devices  7.33 us (2%)
    pallas_call x2, Pallas kernels, swap(): pl.pallas_call(functools.partial(swap_kernel, n_half, n_col, slots, direc...  311 us
    pallas_call x1, Pallas kernels, fold(): pl.pallas_call(functools.partial(fold_kernel, n_row), in_specs=[pl.BlockS...  40 us
    pallas_call x1, Pallas kernels, combine(): pl.pallas_call(combine_kernel, grid_spec=pltpu.PrefetchScalarGridSpec(num...  17 us
    gather x1, local copies, waits for them, and re-layouts, body(): send = child_tiles[picked]  12.8 us
  transfers between devices with their start and end apart: 1, of which 0 were waited for; matrix products, arithmetic and copies ran while one was open for 3% of the time, Pallas kernels for 0%

profile of v3, /device:TPU:0, one launch (start us, length us, event | category | flops | bytes accessed | tf_op | source)
XLA Modules:
  0.0 407.7 jit_solution(10065361535754199285)
XLA Ops:
  1.3 0.9 convert_reduce_fusion.2
  2.2 0.7 compare_and_fusion
  2.9 0.9 convert_reduce_fusion.1
  3.8 0.7 broadcast_add_fusion.1
  4.5 0.7 select_select_fusion
  5.1 0.1 select_reduce_fusion.2
  5.3 0.1 add.141
  5.4 0.1 convert_reduce_fusion.4
  5.5 0.1 pad.4.clone
  5.6 0.6 pad_add_fusion
  6.2 7.3 %all-to-all-start = ((s32[32,1,24]{2,1,0:T(1,128)}), s32[32,1,24]{2,1,0:T(1,128)S(1)}, u32[]{:S(2)}, u32[]{:S(2)}) async-start(s32[32,1,24]{2,1,0:T(1,128)} %bitcast.2), calls=%async_computation | async-start | bytes 32768 | tf_op jit(solution)/shard_map/all_to_all | solution.py:386
  13.6 12.8 %gather_fusion = bf16[256,2,128,128]{3,2,1,0:T(8,128)(2,1)} fusion(bf16[128,2,128,128]{3,2,1,0:T(8,128)(2,1)} %param.12, s32[1024]{0:T(1024)S(1)} %pad_clamp_fusion.1), kind=kCustom, calls=%fused_computation | custom fusion | bytes 33555456 | tf_op jit(solution)/shard_map/gather | solution.py:387
  26.4 0.1 fusion.4
  26.5 0.1 reshape.204
  26.6 0.1 reshape.203
  26.6 0.1 reshape.202
  26.7 0.1 pad_add_fusion.1
  26.8 0.2 convert_reduce_fusion
  27.0 0.7 select_reduce_fusion
  27.7 0.7 convert_reduce_fusion.3.bounds
  28.5 0.2 select_reduce_fusion.4
  28.6 0.6 reduce_max.9
  31.9 0.1 select_reduce_fusion.5
  32.0 0.1 add_select_fusion
  32.1 0.1 select_n.143
  32.2 249.2 %conditional.1 = ((bf16[128,2,128,128]{3,2,1,0:T(8,128)(2,1)}, bf16[64,2,128,128]{3,2,1,0:T(8,128)(2,1)}, bf16[64,2,128,128]{3,2,1,0:T(8,128)(2,1)})) conditional(s32[]{:T(128)} %clamp.3, bf16[256,2,128,128]{3,2,1,0:T(8,128)(2,1)} %gather_fusion, bf16[256,2,128,128]{3,2,1,0:T(8,128)(2,1)} %gather_fusion, ...), branch_computations={%region_11.12_spmd, %region_12.13_spmd, %region_13.14_spmd, %regio... | conditional | bytes 8 | solution.py:391
  32.2 249.2 %branch_0_fun.1 = (bf16[128,2,128,128]{3,2,1,0:T(8,128)(2,1)}, bf16[64,2,128,128]{3,2,1,0:T(8,128)(2,1)}, bf16[64,2,128,128]{3,2,1,0:T(8,128)(2,1)}) custom-call(bf16[256,2,128,128]{3,2,1,0:T(8,128)(2,1)} %refs_0_), custom_call_target="tpu_custom_call" | custom-call | tf_op jit(solution)/shard_map/cond/branch_0_fun/pallas_call | solution.py:237
  281.4 5.3 %gather_fusion.1 = bf16[64,2,128,128]{3,2,1,0:T(8,128)(2,1)} fusion(bf16[64,2,128,128]{3,2,1,0:T(8,128)(2,1)} %get-tuple-element.14, s32[1024]{0:T(1024)S(1)} %pad_clamp_fusion), kind=kCustom, calls=%fused_computation.1 | custom fusion | bytes 8388864 | tf_op jit(solution)/shard_map/gather | solution.py:413
  286.7 62.2 %shard_map.77.passed = bf16[64,2,128,128]{3,2,1,0:T(8,128)(2,1)} custom-call(bf16[64,2,128,128]{3,2,1,0:T(8,128)(2,1)} %gather_fusion.1), custom_call_target="tpu_custom_call" | custom-call | tf_op jit(solution)/shard_map/pallas_call | solution.py:237
  348.9 17.0 %shard_map.78 = (bf16[2,2048,768]{2,1,0:T(8,128)(2,1)}, bf16[8,2,64,768]{3,2,1,0:T(8,128)(2,1)}) custom-call(s32[256]{0:T(256)} %get-tuple-element.20.order, s32[256]{0:T(256)} %get-tuple-element.19.spots, s32[9]{0:T(128)} %convert_reduce_fusion.3.bounds, bf16[2,2048,768]{2,1,0:T(8,128)(2,1)} %front.1, bf16[2,2048,512]{2,1,0:T(8,128)(2,1)} %panel.1, ...), custom_call_target="tpu_custom_call" | custom-call | tf_op jit(solution)/shard_map/pallas_call | solution.py:94
  365.9 40.0 %shard_map.79 = f32[2,64,768]{2,1,0:T(8,128)} custom-call(bf16[8,2,64,768]{3,2,1,0:T(8,128)(2,1)} %get-tuple-element.16.part), custom_call_target="tpu_custom_call" | custom-call | tf_op jit(solution)/shard_map/pallas_call | solution.py:318
  405.9 1.8 copy.25
  (10 shorter events, 0.0 us)
Async XLA Ops:
  6.2 20.2 %all-to-all-start = ((s32[32,1,24]{2,1,0:T(1,128)}), s32[32,1,24]{2,1,0:T(1,128)S(1)}, u32[]{:S(2)}, u32[]{:S(2)}) async-start(s32[32,1,24]{2,1,0:T(1,128)} %bitcast.2), calls=%async_computation | async-start | bytes 32768 | tf_op jit(solution)/shard_map/all_to_all | solution.py:386
